TPU v7x, 512 devices: a whole 4x4x16 slice. The times are simulated.
512 devices in a mesh: domain: 64 (over x, y, z_lo), member: 8 (over z_hi, core).
Axes of the slice: x: 4, y: 4, z: 16 (z_hi: 4, z_lo: 4; z = z_hi * 4 + z_lo), core: 2. Of those that a mesh axis runs over, the one named last changes fastest.
Arguments:
- inputs: bfloat16 [16, 12288, 1024], P('member', 'domain')
- norm_gain: bfloat16 [1024], P('member'), may hold values from 0.099609375 to 1.8984375
- w_query: bfloat16 [1024, 512], P('member')
- w_key: bfloat16 [1024, 512], P('member')
- w_value: bfloat16 [1024, 512], P('member'), may hold values from -0.1875 to 0.1875
- w_out: bfloat16 [512, 1024], P('member'), may hold values from -0.75 to 0.75
- neighbors: int32 [192, 9], P('domain'), may hold values from 0 to 191, as said below
- slot_valid: int32 [192, 9], P('domain'), may hold values from 0 to 1, as said below
- output_cotangent: bfloat16 [16, 12288, 1024], P('member', 'domain'), may hold values from -1.5 to 1.5
Outputs:
- attn_out: bfloat16 [16, 12288, 1024], P('member', 'domain')
- d_input: bfloat16 [16, 12288, 1024], P('member', 'domain')
- grad_wout: float32 [512, 1024], P('member')
Inputs may be any that keep to these rules, and one draw needn't show every extreme that they name: `neighbors`: slot 0 of block b names b. The blocks named by the valid slots of b are distinct and lie within blocks (b // 3 - 1) * 3 to (b // 3 + 2) * 3 - 1. An invalid slot names b. `slot_valid`: slot 0 is always 1.
All inputs are finite; a program needn't handle non-finite values.
Results may differ from a plain program's by a relative error of at most 0.019.
Values may be sent and summed in bfloat16 or wider, within the bound.
No kernel may reach another device: no remote copies, remote signals or barrier semaphores. Data moves between devices by JAX's collectives and lax.ppermute only.
A program may use at most 128 MiB of HBM per device.

v0:
```python
import jax
import jax.numpy as jnp
from jax import lax
from jax.sharding import PartitionSpec as P

HEAD_DIM = 64
EPSILON = 1e-06
MASKED = -1e30


def extended_2(value, sides, width):
    for axis, dim in sides:
        peers, length = (lax.axis_size(axis), value.shape[dim])
        up = [(i, (i + 1) % peers) for i in range(peers - 1)]
        down = [(j, i) for i, j in up]
        last = lax.slice_in_dim(value, length - width, length, axis=dim)
        initial = lax.slice_in_dim(value, 0, width, axis=dim)
        before = lax.ppermute(last, axis, up)
        after = lax.ppermute(initial, axis, down)
        value = jnp.concatenate([before, value, after], axis=dim)
    return value


def pair_columns(field, pair_index, pair_width):
    return lax.dynamic_slice_in_dim(field, pair_index * pair_width, pair_width, field.ndim - 1)


def shards(
    inputs, norm_gain, w_query, w_key, w_value, w_out, neighbors, slot_valid, output_cotangent
):
    samples, length, model_width = inputs.shape
    block_count, slot_count = neighbors.shape
    block_len = length // block_count
    window_blocks = 3 * block_count
    full_gain, complete_query, complete_key, complete_value, complete_output = (
        lax.all_gather(norm_gain, "member", axis=0, tiled=True),
        lax.all_gather(w_query, "member", axis=0, tiled=True),
        lax.all_gather(w_key, "member", axis=0, tiled=True),
        lax.all_gather(w_value, "member", axis=0, tiled=True),
        lax.all_gather(w_out, "member", axis=0, tiled=True),
    )
    hidden_width = complete_query.shape[1]
    pair_width = 2 * HEAD_DIM
    pair_count = hidden_width // pair_width
    score_scale = HEAD_DIM ** (-0.5)
    inputs_float = inputs.astype(jnp.float32)
    inverse_rms = lax.rsqrt(jnp.mean(inputs_float * inputs_float, axis=-1, keepdims=True) + EPSILON)
    gain_float = full_gain.astype(jnp.float32)
    normalized_input = (inputs_float * inverse_rms * gain_float).astype(jnp.bfloat16)
    query = jnp.einsum(
        "fbi,iy->fby", normalized_input, complete_query, preferred_element_type=jnp.float32
    ).astype(jnp.bfloat16)
    key_rows = jnp.einsum(
        "fbi,iy->fby", normalized_input, complete_key, preferred_element_type=jnp.float32
    ).astype(jnp.bfloat16)
    value_rows = jnp.einsum(
        "fbi,iy->fby", normalized_input, complete_value, preferred_element_type=jnp.float32
    ).astype(jnp.bfloat16)
    key_value = jnp.concatenate([key_rows, value_rows], axis=-1)
    extended = extended_2(key_value, (("domain", 1),), length)
    domain_rank = lax.axis_index("domain")
    local_index = neighbors - (domain_rank - 1) * block_count
    present = slot_valid > 0
    window_ids = jnp.arange(window_blocks, dtype=jnp.int32)
    key_all = extended[..., :hidden_width]
    value_all = extended[..., hidden_width:]
    score_spec = "sbqgd,skgd->sbgqk"
    mix_spec = "sbgqk,skgd->sbqgd"
    back_spec = "sbgqk,sbqgd->skgd"
    matches = jnp.logical_and(
        local_index[:, :, None] == window_ids[None, None, :], present[:, :, None]
    )
    included = jnp.any(matches, axis=1)
    key_mask = jnp.repeat(included, block_len, axis=1)

    def pair_keys(pair_index):
        key_pair = pair_columns(key_all, pair_index, pair_width).reshape(
            samples, window_blocks * block_len, 2, HEAD_DIM
        )
        value_pair = pair_columns(value_all, pair_index, pair_width).reshape(
            samples, window_blocks * block_len, 2, HEAD_DIM
        )
        return (key_pair, value_pair)

    def to_window(grad_keys):
        return grad_keys.reshape(samples, window_blocks * block_len, pair_width)

    def pair_probability(pair_index):
        query_pair = pair_columns(query, pair_index, pair_width).reshape(
            samples, block_count, block_len, 2, HEAD_DIM
        )
        key_pair, value_pair = pair_keys(pair_index)
        scores = (
            jnp.einsum(score_spec, query_pair, key_pair, preferred_element_type=jnp.float32)
            * score_scale
        )
        scores = jnp.where(key_mask[None, :, None, None, :], scores, MASKED)
        row_max = jnp.max(scores, axis=-1, keepdims=True)
        shifted = jnp.exp(scores - row_max)
        probability = shifted / jnp.sum(shifted, axis=-1, keepdims=True)
        return (query_pair, key_pair, value_pair, probability)

    def forward_pair(pair_index):
        query_pair, key_pair, value_pair, probability = pair_probability(pair_index)
        prob_bf = probability.astype(jnp.bfloat16)
        mixed_pair = jnp.einsum(mix_spec, prob_bf, value_pair, preferred_element_type=jnp.float32)
        return mixed_pair.astype(jnp.bfloat16).reshape(samples, length, pair_width)

    attention_pairs = lax.map(forward_pair, jnp.arange(pair_count))
    neighbour_attention = jnp.transpose(attention_pairs, (1, 2, 0, 3)).reshape(
        samples, length, hidden_width
    )
    attn_out = jnp.einsum(
        "qny,yb->qnb", neighbour_attention, complete_output, preferred_element_type=jnp.float32
    ).astype(jnp.bfloat16)
    d_attention = jnp.einsum(
        "yjz,bz->yjb", output_cotangent, complete_output, preferred_element_type=jnp.float32
    ).astype(jnp.bfloat16)
    row_share = hidden_width // lax.axis_size("member")
    member_total = samples * lax.axis_size("member")
    incomplete_gradient = jnp.einsum(
        "rfe,rfu->eu", neighbour_attention, output_cotangent, preferred_element_type=jnp.float32
    )
    total_grad = lax.psum(incomplete_gradient, ("domain", "member"))
    grad_mine = lax.dynamic_slice_in_dim(
        total_grad, lax.axis_index("member") * row_share, row_share, 0
    )
    grad_wout = grad_mine / member_total

    def backward_pair(pair_index):
        query_pair, key_pair, value_pair, probability = pair_probability(pair_index)
        prob_bf = probability.astype(jnp.bfloat16)
        grad_pair = pair_columns(d_attention, pair_index, pair_width).reshape(
            samples, block_count, block_len, 2, HEAD_DIM
        )
        d_prob = jnp.einsum(score_spec, grad_pair, value_pair, preferred_element_type=jnp.float32)
        delta = jnp.sum(probability * d_prob, axis=-1, keepdims=True)
        d_score = (probability * (d_prob - delta) * score_scale).astype(jnp.bfloat16)
        d_query_pair = jnp.einsum(mix_spec, d_score, key_pair, preferred_element_type=jnp.float32)
        d_query_pair = d_query_pair.astype(jnp.bfloat16).reshape(samples, length, pair_width)
        d_key_pair = jnp.einsum(back_spec, d_score, query_pair, preferred_element_type=jnp.float32)
        d_value_pair = jnp.einsum(back_spec, prob_bf, grad_pair, preferred_element_type=jnp.float32)
        return (d_query_pair, to_window(d_key_pair), to_window(d_value_pair))

    query_grads, key_grads, value_grads = lax.map(backward_pair, jnp.arange(pair_count))
    query_cotangent = jnp.transpose(query_grads, (1, 2, 0, 3)).reshape(
        samples, length, hidden_width
    )
    key_ext = jnp.transpose(key_grads, (1, 2, 0, 3)).reshape(samples, 3 * length, hidden_width)
    value_ext = jnp.transpose(value_grads, (1, 2, 0, 3)).reshape(samples, 3 * length, hidden_width)
    ext_grad = jnp.concatenate([key_ext, value_ext], axis=-1)
    lower_rim = ext_grad[:, :length]
    own_part = ext_grad[:, length : 2 * length]
    upper_rim = ext_grad[:, 2 * length :]
    rims_half = jnp.concatenate([lower_rim, upper_rim], axis=1).astype(jnp.bfloat16)
    returned = extended_2(rims_half, (("domain", 1),), length)
    from_below = returned[:, :length].astype(jnp.float32)
    from_above = returned[:, 3 * length :].astype(jnp.float32)
    kv_total = own_part + from_below + from_above
    kv_grad = kv_total.astype(jnp.bfloat16)
    key_cotangent = kv_grad[..., :hidden_width]
    value_cotangent = kv_grad[..., hidden_width:]
    normed_cotangent = jnp.einsum(
        "qja,ga->qjg", query_cotangent, complete_query, preferred_element_type=jnp.float32
    )
    normed_cotangent = normed_cotangent + jnp.einsum(
        "qja,ga->qjg", key_cotangent, complete_key, preferred_element_type=jnp.float32
    )
    normed_cotangent = normed_cotangent + jnp.einsum(
        "qja,ga->qjg", value_cotangent, complete_value, preferred_element_type=jnp.float32
    )
    scaled_grad = normed_cotangent * gain_float
    inner_mean = jnp.mean(scaled_grad * inputs_float, axis=-1, keepdims=True)
    d_input = inverse_rms * scaled_grad - inputs_float * inverse_rms**3 * inner_mean
    return (attn_out, d_input.astype(jnp.bfloat16), grad_wout)


def solution(mesh):
    placed = (
        P("member", "domain", None),
        P("member"),
        P("member", None),
        P("member", None),
        P("member", None),
        P("member", None),
        P("domain", None),
        P("domain", None),
        P("member", "domain", None),
    )
    return jax.shard_map(
        shards,
        mesh=mesh,
        in_specs=placed,
        out_specs=(P("member", "domain", None), P("member", "domain", None), P("member", None)),
        check_vma=False,
    )
```

profile of v0, /device:TPU:1, one launch (start us, length us, event | category | flops | bytes accessed | tf_op | source)
XLA Modules:
  0.0 901.7 jit_solution(3319372591805515954)
XLA Ops:
  11.5 22.8 %all-gather = bf16[8,1,128]{2,1,0:T(2,128)(2,1)S(1)} all-gather(bf16[1,1,128]{2,1,0:T(2,128)(2,1)} %bitcast.205), channel_id=1, replica_groups=mesh['domain'=64,'member'=8] {'member'}, dimensions={0}, use_global_device_ids=true | all-gather | bytes 2304 | tf_op jit(solution)/shard_map/all_gather | solution.py:36
  35.0 28.1 %all-gather.8.cloned.1.call-done = bf16[1024,512]{1,0:T(8,128)(2,1)} async-done(((bf16[128,512]{1,0:T(8,128)(2,1)}), bf16[1024,512]{1,0:T(8,128)(2,1)}) %all-gather.8.cloned.1.call-update) | async-done | bytes 1048592 | tf_op jit(solution)/shard_map/all_gather | solution.py:39
  65.2 42.2 %all-gather.6.cloned.1.call-done = bf16[1024,512]{1,0:T(8,128)(2,1)} async-done(((bf16[128,512]{1,0:T(8,128)(2,1)}), bf16[1024,512]{1,0:T(8,128)(2,1)}) %all-gather.6.cloned.1.call-update) | async-done | bytes 1048592 | tf_op jit(solution)/shard_map/all_gather | solution.py:38
  111.5 4.9 collective-permute-start
  116.7 37.4 %all-gather.12.cloned.1.call-done = bf16[512,1024]{1,0:T(8,128)(2,1)} async-done(((bf16[64,1024]{1,0:T(8,128)(2,1)}), bf16[512,1024]{1,0:T(8,128)(2,1)}) %all-gather.12.cloned.1.call-update) | async-done | bytes 1048592 | tf_op jit(solution)/shard_map/all_gather | solution.py:40
  154.0 2.6 convolution_convert_fusion.2
  156.6 59.6 %all-gather.10.cloned.1.call-done = bf16[1024,512]{1,0:T(8,128)(2,1)} async-done(((bf16[128,512]{1,0:T(8,128)(2,1)}), bf16[1024,512]{1,0:T(8,128)(2,1)}) %all-gather.10.cloned.1.call-update) | async-done | bytes 1048592 | tf_op jit(solution)/shard_map/all_gather | solution.py:37
  216.2 2.6 convolution_convert_fusion.3
  224.2 34.7 %while.26 = (s32[]{:T(128)}, bf16[4,2,192,128]{3,2,1,0:T(8,128)(2,1)}, s32[4]{0:T(128)S(1)}, bf16[2,576,512]{1,2,0:T(8,128)(2,1)}, bf16[2,576,512]{1,2,0:T(8,128...) while((s32[]{:T(128)}, ...), condition=%wide.region_5.6_spmd.clone, body=%wide.region_2.5_spmd.clone.sunk | while | flops 117278592 | bytes 8469142 | solution.py:109
  259.7 121.8 %while.27 = (s32[]{:T(128)}, bf16[4,2,192,128]{3,2,1,0:T(8,128)(2,1)}, f32[4,2,576,128]{2,3,1,0:T(8,128)}, f32[4,2,576,128]{2,3,1,0:T(8,128)}, s32[4]{0:T(128)S(...) while((s32[]{:T(128)}, ...), condition=%wide.region_10.11_spmd.clone, body=%wide.region_6.0_spmd.clone.sunk | while | flops 293343744 | bytes 26301140 | solution.py:145
  269.1 7.8 fusion.143
  278.8 2.4 fusion.144
  281.2 7.7 fusion.145
  299.5 7.8 fusion.143
  309.2 2.4 fusion.144
  311.6 7.7 fusion.145
  329.9 7.8 fusion.143
  339.6 2.4 fusion.144
  342.0 7.7 fusion.145
  360.4 7.8 fusion.143
  370.1 2.4 fusion.144
  372.5 7.7 fusion.145
  381.4 3.2 copy.65
  386.8 3.5 constant_dynamic-update-slice_fusion.5
  390.2 2.6 copy.66
  392.8 2.7 reshape.82
  397.3 2.7 convert.6
  402.3 4.9 collective-permute-start.2
  409.3 2.8 convolution_convert_fusion.1
  412.7 9.3 %collective-permute-done.3 = bf16[2,192,1024]{2,1,0:T(8,128)(2,1)} collective-permute-done((bf16[2,192,1024]{2,1,0:T(8,128)(2,1)}, bf16[2,192,1024]{2,1,0:T(8,128)(2,1)}, u32[]{:S(2)}, u32[]{:S(2)}) %collective-permute-start.3) | collective-permute-done | bytes 786464 | tf_op jit(solution)/shard_map/ppermute | solution.py:19
  422.6 2.2 fusion.58
  428.5 465.0 %all-reduce.2.cloned.1.call-done = f32[512,1024]{1,0:T(8,128)} async-done(((f32[512,1024]{1,0:T(8,128)}), f32[512,1024]{1,0:T(8,128)}) %all-reduce.2.cloned.1.call-update) | async-done | bytes 2097168 | tf_op jit(solution)/shard_map/psum | solution.py:124
  (198 shorter events, 111.2 us)
Async XLA Ops:
  7.2 146.9 %copy-start = (bf16[2,192,1024]{2,1,0:T(8,128)(2,1)S(1)}, bf16[2,192,1024]{2,1,0:T(8,128)(2,1)}, u32[]{:S(2)}) copy-start(bf16[2,192,1024]{2,1,0:T(8,128)(2,1)} %param.21) | copy-start | bytes 2359300
  7.2 55.9 %all-gather.8.cloned.1.call-start = ((), (), s32[]{:S(2)}) async-start(), calls=%async_computation.1 | async-start | bytes 1179648 | tf_op jit(solution)/shard_map/all_gather | solution.py:39
  7.9 99.4 %all-gather.6.cloned.1.call-start = ((), (), s32[]{:S(2)}) async-start(), calls=%async_computation | async-start | bytes 1179648 | tf_op jit(solution)/shard_map/all_gather | solution.py:38
  8.7 145.4 %all-gather.12.cloned.1.call-start = ((), (), s32[]{:S(2)}) async-start(), calls=%async_computation.3 | async-start | bytes 1179648 | tf_op jit(solution)/shard_map/all_gather | solution.py:40
  9.4 206.8 %all-gather.10.cloned.1.call-start = ((), (), s32[]{:S(2)}) async-start(), calls=%async_computation.2 | async-start | bytes 1179648 | tf_op jit(solution)/shard_map/all_gather | solution.py:37
  10.0 97.4 %copy-start.2 = (bf16[2,192,1024]{2,1,0:T(8,128)(2,1)S(1)}, bf16[2,192,1024]{2,1,0:T(8,128)(2,1)}, u32[]{:S(2)}) copy-start(bf16[2,192,1024]{2,1,0:T(8,128)(2,1)} %param.13) | copy-start | bytes 2359300
  10.0 883.5 %all-reduce.2.cloned.1.call-start = ((), (), s32[]{:S(2)}) async-start(), calls=%async_computation.4 | async-start | bytes 4194304 | tf_op jit(solution)/shard_map/psum | solution.py:124
  65.1 51.2 %copy-start.10 = (s32[3,9]{1,0:T(4,128)S(1)}, s32[3,9]{1,0:T(4,128)}, u32[]{:S(2)}) copy-start(s32[3,9]{1,0:T(4,128)} %param.20) | copy-start | bytes 328
  110.2 108.6 %collective-permute-start.1 = (bf16[2,192,1024]{2,1,0:T(8,128)(2,1)}, bf16[2,192,1024]{2,1,0:T(8,128)(2,1)S(1)}, u32[]{:S(2)}, u32[]{:S(2)}) collective-permute-start(bf16[2,192,1024]{2,1,0:T(8,128)(2,1)} %pad_maximum_fusion.1), channel_id=1, source_target_pairs={{8,0},{16,8},{24,16},{32,24},{40,32},{48,40},{56,48},{64,56},{72,6... | collective-permute-start | bytes 2359304 | tf_op jit(solution)/shard_map/ppermute | solution.py:19
  111.5 107.3 %collective-permute-start = (bf16[2,192,1024]{2,1,0:T(8,128)(2,1)}, bf16[2,192,1024]{2,1,0:T(8,128)(2,1)}, u32[]{:S(2)}, u32[]{:S(2)}) collective-permute-start(bf16[2,192,1024]{2,1,0:T(8,128)(2,1)} %pad_maximum_fusion.1), channel_id=1, source_target_pairs={{0,8},{8,16},{16,24},{24,32},{32,40},{40,48},{48,56},{56,64},{64,7... | collective-permute-start | bytes 2359304 | tf_op jit(solution)/shard_map/ppermute | solution.py:18
  281.2 7.7 copy-start.1
  311.6 7.7 copy-start.1
  342.0 7.7 copy-start.1
  372.5 7.7 copy-start.1
  386.8 3.5 copy-start.4
  400.0 7.2 copy-start.5
  401.0 21.0 %collective-permute-start.3 = (bf16[2,192,1024]{2,1,0:T(8,128)(2,1)}, bf16[2,192,1024]{2,1,0:T(8,128)(2,1)}, u32[]{:S(2)}, u32[]{:S(2)}) collective-permute-start(bf16[2,192,1024]{2,1,0:T(8,128)(2,1)} %get-tuple-element.247), channel_id=1, source_target_pairs={{8,0},{16,8},{24,16},{32,24},{40,32},{48,40},{56,48},{64,56},{72,6... | collective-permute-start | bytes 2359304 | tf_op jit(solution)/shard_map/ppermute | solution.py:19
  402.3 20.3 %collective-permute-start.2 = (bf16[2,192,1024]{2,1,0:T(8,128)(2,1)S(1)}, bf16[2,192,1024]{2,1,0:T(8,128)(2,1)}, u32[]{:S(2)}, u32[]{:S(2)}) collective-permute-start(bf16[2,192,1024]{2,1,0:T(8,128)(2,1)S(1)} %get-tuple-element.246), channel_id=1, source_target_pairs={{0,8},{8,16},{16,24},{24,32},{32,40},{40,48},{48,56},{56,64},{64,7... | collective-permute-start | bytes 2359304 | tf_op jit(solution)/shard_map/ppermute | solution.py:18
  409.3 2.8 copy-start.6
  409.3 2.8 copy-start.8
  412.7 12.2 %copy-start.7 = (bf16[1024,512]{1,0:T(8,128)(2,1)S(1)}, bf16[1024,512]{1,0:T(8,128)(2,1)}, u32[]{:S(2)}) copy-start(bf16[1024,512]{1,0:T(8,128)(2,1)} %all-gather.6.cloned.1.call-done) | copy-start | bytes 3145732
  424.9 1.1 copy-start.3
  424.9 1.5 copy-start.9
Sparse Core Ops, SparseCore 0:
  10.1 52.8 all-gather.7
  65.2 42.0 all-gather.5
  109.5 44.4 all-gather.11
  156.0 60.1 all-gather.9
  409.4 484.0 all-reduce.1
where the time goes:
time: 903 us; the launch traced here: 902 us
  waiting for transfers between devices  645 us (71%)
  matrix products  106 us (12%)
  local copies, waits for them, and re-layouts  73.6 us (8%)
  blocking collectives  22.8 us (3%)
  other arithmetic  22.2 us (2%)
  between operations  14 us (2%)
  starting transfers between devices  12.5 us (1%)
    psum x1, waiting for transfers between devices, shards(): total_grad = lax.psum(incomplete_gradient, ('domain', 'member'))  465 us
    all_gather x1, waiting for transfers between devices, shards(): lax.all_gather(w_query, 'member', axis=0, tiled=True)  59.6 us
    all_gather x1, waiting for transfers between devices, shards(): lax.all_gather(w_key, 'member', axis=0, tiled=True)  42.2 us
    all_gather x1, waiting for transfers between devices, shards(): lax.all_gather(w_out, 'member', axis=0, tiled=True)  37.4 us
    dot_general x4, matrix products, backward_pair(): jnp.einsum(mix_spec, d_score, key_pair, preferred_element_type=jnp.float32)  31.3 us
    dot_general x4, matrix products, backward_pair(): jnp.einsum(back_spec, d_score, query_pair, preferred_element_type=jnp.flo...  30.7 us
    all_gather x1, waiting for transfers between devices, shards(): lax.all_gather(w_value, 'member', axis=0, tiled=True)  28.1 us
    dynamic_slice x24, local copies, waits for them, and re-layouts, pair_columns(): lax.dynamic_slice_in_dim(field, pair_index * pair_width, pair_width, fiel...  23.5 us
  transfers between devices with their start and end apart: 9, of which 7 were waited for; matrix products, arithmetic and copies ran while one was open for 3% of the time, Pallas kernels for 0%

commit v1 on v0

--- a/solution.py
+++ b/solution.py
@@ -35,7 +35,12 @@
     full_gain, complete_query, complete_key, complete_value, complete_output = (
         lax.all_gather(norm_gain, "member", axis=0, tiled=True),
         lax.all_gather(w_query, "member", axis=0, tiled=True),
-        lax.all_gather(w_key, "member", axis=0, tiled=True),
+        jnp.concatenate(
+            lax.all_to_all(
+                jnp.stack([w_key] * lax.axis_size("member")), "member", split_axis=0, concat_axis=0
+            ),
+            axis=0,
+        ),
         lax.all_gather(w_value, "member", axis=0, tiled=True),
         lax.all_gather(w_out, "member", axis=0, tiled=True),
     )

time: 903 us -> 899 us (level)
  waiting for transfers between devices: 645 us -> 582 us
  blocking collectives: 22.8 us -> 67.3 us
  starting transfers between devices: 12.5 us -> 28.2 us
    all_gather x1, blocking collectives: 22.8 us -> 67.3 us  [shards(): lax.all_gather(norm_gain, 'member', axis=0, tiled=True)]
    all_gather x1 -> x0, waiting for transfers between devices: 42.2 us -> none  [shards(): lax.all_gather(w_key, 'member', axis=0, tiled=True)]
    all_gather x1, waiting for transfers between devices: 28.1 us -> 2.62 us  [shards(): lax.all_gather(w_value, 'member', axis=0, tiled=True)]
    all_to_all x0 -> x1, starting transfers between devices: none -> 16.6 us  [shards(): lax.all_to_all(jnp.stack([w_key] * lax.axis_size('member')), 'member', sp...]
  transfers between devices with their start and end apart: 9 -> 9, of which waited for: 7 -> 6; matrix products, arithmetic and copies ran while one was open for 3% -> 2% of each run, Pallas kernels for 0% -> 0%
where the time goes in v1:
time: 899 us; the launch traced here: 898 us
  waiting for transfers between devices  582 us (65%)
  matrix products  105 us (12%)
  local copies, waits for them, and re-layouts  75.7 us (8%)
  blocking collectives  67.3 us (7%)
  starting transfers between devices  28.2 us (3%)
  other arithmetic  20.3 us (2%)
  between operations  14 us (2%)
    psum x1, waiting for transfers between devices, shards(): total_grad = lax.psum(incomplete_gradient, ('domain', 'member'))  465 us
    all_gather x1, blocking collectives, shards(): lax.all_gather(norm_gain, 'member', axis=0, tiled=True)  67.3 us
    all_gather x1, waiting for transfers between devices, shards(): lax.all_gather(w_query, 'member', axis=0, tiled=True)  64.4 us
    all_gather x1, waiting for transfers between devices, shards(): lax.all_gather(w_out, 'member', axis=0, tiled=True)  37.4 us
    dot_general x4, matrix products, backward_pair(): jnp.einsum(mix_spec, d_score, key_pair, preferred_element_type=jnp.float32)  31.3 us
    dot_general x4, matrix products, backward_pair(): jnp.einsum(back_spec, d_score, query_pair, preferred_element_type=jnp.flo...  30.7 us
    dynamic_slice x24, local copies, waits for them, and re-layouts, pair_columns(): lax.dynamic_slice_in_dim(field, pair_index * pair_width, pair_width, fiel...  23.5 us
  transfers between devices with their start and end apart: 9, of which 6 were waited for; matrix products, arithmetic and copies ran while one was open for 2% of the time, Pallas kernels for 0%

profile of v1, /device:TPU:1, one launch (start us, length us, event | category | flops | bytes accessed | tf_op | source)
XLA Modules:
  0.0 897.7 jit_solution(2861220251312943029)
XLA Ops:
  10.0 16.6 %all-to-all-start = ((bf16[8,128,512]{2,1,0:T(8,128)(2,1)}), bf16[8,128,512]{2,1,0:T(8,128)(2,1)S(1)}, u32[]{:S(2)}, u32[]{:S(2)}) async-start(bf16[8,128,512]{2,1,0:T(8,128)(2,1)} %stack.2), calls=%async_computation | async-start | bytes 2097152 | tf_op jit(solution)/shard_map/all_to_all | solution.py:39
  28.3 67.3 %all-gather = bf16[8,1,128]{2,1,0:T(2,128)(2,1)S(1)} all-gather(bf16[1,1,128]{2,1,0:T(2,128)(2,1)S(1)} %bitcast.207), channel_id=1, replica_groups=mesh['domain'=64,'member'=8] {'member'}, dimensions={0}, use_global_device_ids=true | all-gather | bytes 2304 | tf_op jit(solution)/shard_map/all_gather | solution.py:36
  95.6 2.6 all-gather.5.cloned.1.call-done
  103.0 4.0 collective-permute-start
  107.4 37.4 %all-gather.9.cloned.1.call-done = bf16[512,1024]{1,0:T(8,128)(2,1)} async-done(((bf16[64,1024]{1,0:T(8,128)(2,1)}), bf16[512,1024]{1,0:T(8,128)(2,1)}) %all-gather.9.cloned.1.call-update) | async-done | bytes 1048592 | tf_op jit(solution)/shard_map/all_gather | solution.py:45
  144.8 2.6 convolution_convert_fusion.2
  147.4 64.4 %all-gather.7.cloned.1.call-done = bf16[1024,512]{1,0:T(8,128)(2,1)} async-done(((bf16[128,512]{1,0:T(8,128)(2,1)}), bf16[1024,512]{1,0:T(8,128)(2,1)}) %all-gather.7.cloned.1.call-update) | async-done | bytes 1048592 | tf_op jit(solution)/shard_map/all_gather | solution.py:37
  211.8 2.6 convolution_convert_fusion.3
  219.8 34.7 %while.26 = (s32[]{:T(128)}, bf16[4,2,192,128]{3,2,1,0:T(8,128)(2,1)}, s32[4]{0:T(128)S(1)}, bf16[2,576,512]{1,2,0:T(8,128)(2,1)}, bf16[2,576,512]{1,2,0:T(8,128...) while((s32[]{:T(128)}, ...), condition=%wide.region_5.6_spmd.clone, body=%wide.region_2.5_spmd.clone.sunk | while | flops 117278592 | bytes 8469142 | solution.py:114
  255.3 121.7 %while.27 = (s32[]{:T(128)}, bf16[4,2,192,128]{3,2,1,0:T(8,128)(2,1)}, f32[4,2,576,128]{2,3,1,0:T(8,128)}, f32[4,2,576,128]{2,3,1,0:T(8,128)}, s32[4]{0:T(128)S(...) while((s32[]{:T(128)}, ...), condition=%wide.region_10.11_spmd.clone, body=%wide.region_6.0_spmd.clone.sunk | while | flops 293343744 | bytes 26301140 | solution.py:150
  264.7 7.8 fusion.143
  274.4 2.4 fusion.144
  276.8 7.7 fusion.145
  295.1 7.8 fusion.143
  304.8 2.4 fusion.144
  307.2 7.7 fusion.145
  325.5 7.8 fusion.143
  335.2 2.4 fusion.144
  337.6 7.7 fusion.145
  356.0 7.8 fusion.143
  365.7 2.4 fusion.144
  368.1 7.7 fusion.145
  377.0 3.2 copy.65
  382.3 3.5 constant_dynamic-update-slice_fusion.5
  385.8 2.6 copy.66
  388.4 2.7 reshape.88
  392.8 2.7 convert.6
  397.9 4.9 collective-permute-start.2
  404.9 2.8 convolution_convert_fusion.1
  408.3 9.3 %collective-permute-done.3 = bf16[2,192,1024]{2,1,0:T(8,128)(2,1)} collective-permute-done((bf16[2,192,1024]{2,1,0:T(8,128)(2,1)}, bf16[2,192,1024]{2,1,0:T(8,128)(2,1)}, u32[]{:S(2)}, u32[]{:S(2)}) %collective-permute-start.3) | collective-permute-done | bytes 786464 | tf_op jit(solution)/shard_map/ppermute | solution.py:19
  418.2 2.3 fusion.58
  424.0 465.5 %all-reduce.2.cloned.1.call-done = f32[512,1024]{1,0:T(8,128)} async-done(((f32[512,1024]{1,0:T(8,128)}), f32[512,1024]{1,0:T(8,128)}) %all-reduce.2.cloned.1.call-update) | async-done | bytes 2097168 | tf_op jit(solution)/shard_map/psum | solution.py:129
  (204 shorter events, 109.4 us)
Async XLA Ops:
  7.2 137.7 %copy-start = (bf16[2,192,1024]{2,1,0:T(8,128)(2,1)S(1)}, bf16[2,192,1024]{2,1,0:T(8,128)(2,1)}, u32[]{:S(2)}) copy-start(bf16[2,192,1024]{2,1,0:T(8,128)(2,1)} %param.21) | copy-start | bytes 2359300
  7.2 20.9 %copy-start.2 = (bf16[2,192,1024]{2,1,0:T(8,128)(2,1)S(1)}, bf16[2,192,1024]{2,1,0:T(8,128)(2,1)}, u32[]{:S(2)}) copy-start(bf16[2,192,1024]{2,1,0:T(8,128)(2,1)} %param.13) | copy-start | bytes 2359300
  7.2 91.1 %all-gather.5.cloned.1.call-start = ((), (), s32[]{:S(2)}) async-start(), calls=%async_computation.1 | async-start | bytes 1179648 | tf_op jit(solution)/shard_map/all_gather | solution.py:44
  7.9 20.4 %copy-start.13 = (bf16[128]{0:T(256)(128)(2,1)S(1)}, bf16[128]{0:T(256)(128)(2,1)}, u32[]{:S(2)}) copy-start(bf16[128]{0:T(256)(128)(2,1)} %param.14) | copy-start | bytes 772
  7.9 87.7 %copy-start.12 = (s32[3,9]{1,0:T(4,128)S(1)}, s32[3,9]{1,0:T(4,128)}, u32[]{:S(2)}) copy-start(s32[3,9]{1,0:T(4,128)} %param.19) | copy-start | bytes 328
  10.0 90.1 %all-to-all-start = ((bf16[8,128,512]{2,1,0:T(8,128)(2,1)}), bf16[8,128,512]{2,1,0:T(8,128)(2,1)S(1)}, u32[]{:S(2)}, u32[]{:S(2)}) async-start(bf16[8,128,512]{2,1,0:T(8,128)(2,1)} %stack.2), calls=%async_computation | async-start | bytes 2097152 | tf_op jit(solution)/shard_map/all_to_all | solution.py:39
  26.6 118.3 %all-gather.9.cloned.1.call-start = ((), (), s32[]{:S(2)}) async-start(), calls=%async_computation.3 | async-start | bytes 1179648 | tf_op jit(solution)/shard_map/all_gather | solution.py:45
  27.3 184.5 %all-gather.7.cloned.1.call-start = ((), (), s32[]{:S(2)}) async-start(), calls=%async_computation.2 | async-start | bytes 1179648 | tf_op jit(solution)/shard_map/all_gather | solution.py:37
  28.0 861.5 %all-reduce.2.cloned.1.call-start = ((), (), s32[]{:S(2)}) async-start(), calls=%async_computation.4 | async-start | bytes 4194304 | tf_op jit(solution)/shard_map/psum | solution.py:129
  100.1 1.6 copy-start.4
  100.1 7.0 copy-start.11
  101.7 112.6 %collective-permute-start.1 = (bf16[2,192,1024]{2,1,0:T(8,128)(2,1)}, bf16[2,192,1024]{2,1,0:T(8,128)(2,1)}, u32[]{:S(2)}, u32[]{:S(2)}) collective-permute-start(bf16[2,192,1024]{2,1,0:T(8,128)(2,1)} %pad_maximum_fusion.1), channel_id=1, source_target_pairs={{8,0},{16,8},{24,16},{32,24},{40,32},{48,40},{56,48},{64,56},{72,6... | collective-permute-start | bytes 2359304 | tf_op jit(solution)/shard_map/ppermute | solution.py:19
  103.0 111.4 %collective-permute-start = (bf16[2,192,1024]{2,1,0:T(8,128)(2,1)}, bf16[2,192,1024]{2,1,0:T(8,128)(2,1)S(1)}, u32[]{:S(2)}, u32[]{:S(2)}) collective-permute-start(bf16[2,192,1024]{2,1,0:T(8,128)(2,1)} %pad_maximum_fusion.1), channel_id=1, source_target_pairs={{0,8},{8,16},{16,24},{24,32},{32,40},{40,48},{48,56},{56,64},{64,7... | collective-permute-start | bytes 2359304 | tf_op jit(solution)/shard_map/ppermute | solution.py:18
  276.8 7.7 copy-start.1
  307.2 7.7 copy-start.1
  337.6 7.7 copy-start.1
  368.1 7.7 copy-start.1
  382.3 3.5 copy-start.6
  395.5 7.2 copy-start.7
  396.6 21.0 %collective-permute-start.3 = (bf16[2,192,1024]{2,1,0:T(8,128)(2,1)}, bf16[2,192,1024]{2,1,0:T(8,128)(2,1)}, u32[]{:S(2)}, u32[]{:S(2)}) collective-permute-start(bf16[2,192,1024]{2,1,0:T(8,128)(2,1)} %get-tuple-element.247), channel_id=1, source_target_pairs={{8,0},{16,8},{24,16},{32,24},{40,32},{48,40},{56,48},{64,56},{72,6... | collective-permute-start | bytes 2359304 | tf_op jit(solution)/shard_map/ppermute | solution.py:19
  397.9 20.3 %collective-permute-start.2 = (bf16[2,192,1024]{2,1,0:T(8,128)(2,1)S(1)}, bf16[2,192,1024]{2,1,0:T(8,128)(2,1)}, u32[]{:S(2)}, u32[]{:S(2)}) collective-permute-start(bf16[2,192,1024]{2,1,0:T(8,128)(2,1)S(1)} %get-tuple-element.246), channel_id=1, source_target_pairs={{0,8},{8,16},{16,24},{24,32},{32,40},{40,48},{48,56},{56,64},{64,7... | collective-permute-start | bytes 2359304 | tf_op jit(solution)/shard_map/ppermute | solution.py:18
  404.8 2.8 copy-start.8
  404.8 2.8 copy-start.9
  408.3 12.2 %copy-start.5 = (bf16[8,128,512]{2,1,0:T(8,128)(2,1)S(1)}, bf16[8,128,512]{2,1,0:T(8,128)(2,1)}, u32[]{:S(2)}) copy-start(bf16[8,128,512]{2,1,0:T(8,128)(2,1)} %copy-done.4) | copy-start | bytes 3145732
  420.4 1.1 copy-start.3
  420.5 1.5 copy-start.10
Sparse Core Ops, SparseCore 0:
  10.2 88.0 all-gather.4
  100.4 44.3 all-gather.8
  147.0 64.7 all-gather.6
  405.0 484.4 all-reduce.1
